TPU v7x, 256 devices: a whole 4x4x8 slice. The times are simulated.
256 devices in a mesh: walker: 64 (over x_hi, y, z), freq: 4 (over x_lo, core).
Axes of the slice: x: 4 (x_hi: 2, x_lo: 2; x = x_hi * 2 + x_lo), y: 4, z: 8, core: 2. Of those that a mesh axis runs over, the one named last changes fastest.
Arguments:
- green_up_blocks: bfloat16 [64, 1, 4, 4288], P('walker', None, 'freq'), may hold values from -6 to 6
- green_down_blocks: bfloat16 [64, 1, 4, 4288], P('walker', None, 'freq'), may hold values from -6 to 6
- nu_index: int32 [4], P('freq'), may hold values from 0 to 3, each once
- q_index: int32 [4], P('freq'), may hold values from 0 to 63
- source: float32 [4, 4096], P('freq', 'walker'), may hold values from -6 to 6
Outputs:
- g4: float32 [4, 4096, 4096], P('freq', 'walker')
- response: float32 [4, 4096], P('freq', 'walker')
All inputs are finite; a program needn't handle non-finite values.
Results may differ from a plain program's by a relative error of at most 0.004.
Values may be sent and summed in bfloat16 or wider, within the bound.
No kernel may reach another device: no remote copies, remote signals or barrier semaphores. Data moves between devices by JAX's collectives and lax.ppermute only.
A program may use at most 64 MiB of HBM per device.

v0:
```python
import math
import jax
import jax.numpy as jnp
from jax import lax
from jax.sharding import PartitionSpec as P

SIDE = 8
CLUSTER_MOMENTUM = 64
W = 64
NU = 4
ITERS = 2


def cluster_sum(sites, shift):
    return (sites // SIDE + shift // SIDE) % SIDE * SIDE + (sites % SIDE + shift % SIDE) % SIDE


def products(block, sites, shift, offset):
    moved = cluster_sum(sites, shift)
    base = jnp.take(block, sites, axis=1)[:, :, :W].astype(jnp.float32)
    other = lax.dynamic_slice_in_dim(jnp.take(block, moved, axis=1), offset, W, 2).astype(
        jnp.float32
    )
    return (base * other).astype(jnp.bfloat16).reshape(block.shape[0], sites.shape[0] * W)


def stacked(block, sites, nu_index, q_index):
    return jnp.stack([products(block, sites, q_index[0], nu_index[0])])


def accumulate(left, right):
    return jnp.einsum("nrk,nrc->nkc", left, right, preferred_element_type=jnp.float32)


def shards(green_up_blocks, green_down_blocks, nu_index, q_index, source):
    up_all, down_all = (
        lax.all_gather(green_up_blocks, "freq", axis=2, tiled=True),
        lax.all_gather(green_down_blocks, "freq", axis=2, tiled=True),
    )
    extent = W + NU - 1
    rows_one = up_all.shape[1] * up_all.shape[2]
    walkers = lax.axis_size("walker")
    per_dev = CLUSTER_MOMENTUM // walkers
    owned = lax.axis_index("walker") * per_dev + jnp.arange(per_dev, dtype=jnp.int32)
    every = jnp.arange(CLUSTER_MOMENTUM, dtype=jnp.int32)

    def blocks(piece):
        return piece.reshape(-1, CLUSTER_MOMENTUM, extent)

    left = stacked(
        blocks(lax.all_gather(up_all, "walker", axis=0, tiled=True)), owned, nu_index, q_index
    )
    right = stacked(
        blocks(lax.all_gather(down_all, "walker", axis=0, tiled=True)), every, nu_index, q_index
    )
    summed = accumulate(left, right)
    kernel = summed * (1.0 / math.sqrt(walkers * rows_one))
    scale = 1.0 / (2.0 * math.sqrt(CLUSTER_MOMENTUM * W))
    start_vec = source.T
    current = start_vec
    for step in range(ITERS):

        def term(begin, sample_count, current=current):
            return jnp.einsum("kn,nkc->cn", current, kernel, precision=lax.Precision.HIGHEST)

        current = start_vec + scale * lax.psum_scatter(
            term(jnp.int32(0), lax.axis_size("walker") * (per_dev * W)),
            "walker",
            scatter_dimension=0,
            tiled=True,
        )
    return (kernel, current.T)


def solution(mesh):
    in_specs = (
        P("walker", None, "freq", None),
        P("walker", None, "freq", None),
        P("freq"),
        P("freq"),
        P("freq", "walker"),
    )
    out_specs = (P("freq", "walker", None), P("freq", "walker"))
    return jax.shard_map(shards, mesh=mesh, in_specs=in_specs, out_specs=out_specs, check_vma=False)
```

profile of v0, /device:TPU:2, one launch (start us, length us, event | category | flops | bytes accessed | tf_op | source)
XLA Modules:
  0.0 1031.1 jit_solution(13348956791322953057)
XLA Ops:
  7.2 0.0 all-gather.3.cloned.1.call-start
  7.2 5.7 all_gather.12
  13.0 0.6 copy.18
  13.6 0.0 all-gather.3.cloned.1.call-update
  13.6 0.0 all-gather.5.cloned.1.call-start
  13.6 5.7 all_gather.14
  19.4 0.6 copy.22
  20.0 0.0 all-gather.5.cloned.1.call-update
  20.0 0.0 reduce-scatter.7.cloned.1.call-start
  21.5 112.9 %all-gather.3.cloned.1.call-done = bf16[64,1,4,4288]{3,2,1,0:T(4,128)(2,1)} async-done(((bf16[1,1,4,4288]{3,2,1,0:T(4,128)(2,1)}), bf16[64,1,4,4288]{3,2,1,0:T(4,128)(2,1)}) %all-gather.3.cloned.1.call-update) | async-done | bytes 2195472 | tf_op jit(solution)/shard_map/all_gather | solution.py:51
  134.4 15.4 %reshape.59 = bf16[256,64,67]{2,1,0:T(8,128)(2,1)} reshape(bf16[64,1,4,4288]{3,2,1,0:T(4,128)(2,1)} %all-gather.3.cloned.1.call-done) | data formatting | bytes 4390912 | tf_op jit(solution)/shard_map/reshape | solution.py:48
  149.9 1.5 constant_dynamic-slice_fusion.1
  151.4 0.2 constant_dynamic-slice_fusion.2
  151.6 0.1 copy.32
  151.7 0.1 copy.31
  151.8 102.3 %all-gather.5.cloned.1.call-done = bf16[64,1,4,4288]{3,2,1,0:T(4,128)(2,1)} async-done(((bf16[1,1,4,4288]{3,2,1,0:T(4,128)(2,1)}), bf16[64,1,4,4288]{3,2,1,0:T(4,128)(2,1)}) %all-gather.5.cloned.1.call-update) | async-done | bytes 2195472 | tf_op jit(solution)/shard_map/all_gather | solution.py:54
  254.1 15.4 %reshape.61 = bf16[256,64,67]{2,1,0:T(8,128)(2,1)} reshape(bf16[64,1,4,4288]{3,2,1,0:T(4,128)(2,1)} %all-gather.5.cloned.1.call-done) | data formatting | bytes 4390912 | tf_op jit(solution)/shard_map/reshape | solution.py:48
  269.5 6.7 copy.23
  276.2 2.1 gather_fusion.1
  278.3 2.1 gather_fusion
  280.4 2.9 select_bitcast_fusion
  283.3 1.3 multiply_convert_fusion
  284.6 0.0 copy-start.1
  284.6 0.8 convolution_multiply_fusion
  285.3 0.0 copy-done.1
  285.3 0.0 copy-start
  285.3 4.8 convolution_bitcast_fusion.1
  290.1 0.0 reduce-scatter.7.cloned.1.call-update
  290.1 0.0 reduce-scatter.9.cloned.1.call-start
  290.2 365.8 %reduce-scatter.7.cloned.1.call-done = f32[64,1]{1,0:T(8,128)} async-done(((f32[4096,1]{1,0:T(8,128)}), f32[64,1]{1,0:T(8,128)}) %reduce-scatter.7.cloned.1.call-update) | async-done | bytes 272
  656.0 0.8 copy.26
  656.9 0.0 copy-done
  656.9 4.8 convolution_bitcast_fusion
  661.6 0.0 reduce-scatter.9.cloned.1.call-update
  661.7 361.6 %reduce-scatter.9.cloned.1.call-done = f32[64,1]{1,0:T(8,128)} async-done(((f32[4096,1]{1,0:T(8,128)}), f32[64,1]{1,0:T(8,128)}) %reduce-scatter.9.cloned.1.call-update) | async-done | bytes 272
  1023.2 0.8 copy.28
  1024.1 0.5 fusion.14
  (5 shorter events, 0.0 us)
Async XLA Ops:
  7.2 127.3 %all-gather.3.cloned.1.call-start = ((), (), s32[]{:S(2)}) async-start(), calls=%async_computation.2 | async-start | bytes 2263040 | tf_op jit(solution)/shard_map/all_gather | solution.py:51
  13.6 240.5 %all-gather.5.cloned.1.call-start = ((), (), s32[]{:S(2)}) async-start(), calls=%async_computation.3 | async-start | bytes 2263040 | tf_op jit(solution)/shard_map/all_gather | solution.py:54
  20.0 636.0 %reduce-scatter.7.cloned.1.call-start = ((), (), s32[]{:S(2)}) async-start(), calls=%async_computation.4 | async-start | bytes 2129920
  284.6 0.8 copy-start.1
  285.3 371.5 %copy-start = (f32[64,4096]{1,0:T(8,128)}, f32[64,4096]{1,0:T(8,128)S(1)}, u32[]{:S(2)}) copy-start(f32[64,4096]{1,0:T(8,128)S(1)} %convolution_multiply_fusion) | copy-start | bytes 3145732
  290.1 733.1 %reduce-scatter.9.cloned.1.call-start = ((), (), s32[]{:S(2)}) async-start(), calls=%async_computation.5 | async-start | bytes 2129920
Sparse Core Ops, SparseCore 0:
  13.7 120.6 all-gather.2
  138.6 115.4 all-gather.4
  290.3 365.7 reduce-scatter.6
  661.8 361.4 reduce-scatter.8
where the time goes:
time: 1030 us
  waiting for transfers between devices  943 us (92%)
  local copies, waits for them, and re-layouts  46.5 us (5%)
  between operations  15.3 us (1%)
  blocking collectives  11.5 us (1%)
  matrix products  10.3 us (1%)
    unnamed x6, waiting for transfers between devices  727 us
    all_gather x1, waiting for transfers between devices, shards(): lax.all_gather(up_all, 'walker', axis=0, tiled=True)  113 us
    all_gather x1, waiting for transfers between devices, shards(): lax.all_gather(down_all, 'walker', axis=0, tiled=True)  102 us
    reshape x3, local copies, waits for them, and re-layouts, blocks(): return piece.reshape(-1, CLUSTER_MOMENTUM, extent)  37.5 us
  transfers between devices with their start and end apart: 4, of which 4 were waited for; matrix products, arithmetic and copies ran while one was open for 2% of the time, Pallas kernels for 0%

commit v1 on v0

--- a/solution.py
+++ b/solution.py
@@ -50,9 +50,13 @@
     left = stacked(
         blocks(lax.all_gather(up_all, "walker", axis=0, tiled=True)), owned, nu_index, q_index
     )
-    right = stacked(
-        blocks(lax.all_gather(down_all, "walker", axis=0, tiled=True)), every, nu_index, q_index
-    )
+
+    def resolve_record_by_axis(mine, comm_axis):
+        far_arr = jnp.stack([mine for _ in range(jax.lax.psum(1, axis_name=comm_axis))])
+        row_out = jax.lax.all_to_all(far_arr, axis_name=comm_axis, split_axis=0, concat_axis=0)
+        return jnp.concatenate(row_out, axis=0)
+
+    right = stacked(blocks(resolve_record_by_axis(down_all, "walker")), every, nu_index, q_index)
     summed = accumulate(left, right)
     kernel = summed * (1.0 / math.sqrt(walkers * rows_one))
     scale = 1.0 / (2.0 * math.sqrt(CLUSTER_MOMENTUM * W))

time: 1030 us -> 923 us (0.90)
  waiting for transfers between devices: 943 us -> 818 us
  starting transfers between devices: 0.16 us -> 14 us
    all_gather x1 -> x0, waiting for transfers between devices: 102 us -> none  [shards(): lax.all_gather(down_all, 'walker', axis=0, tiled=True)]
    all_gather x1, waiting for transfers between devices: 113 us -> 44.5 us  [shards(): lax.all_gather(up_all, 'walker', axis=0, tiled=True)]
    all_to_all x0 -> x1, waiting for transfers between devices: none -> 46 us  [resolve_record_by_axis(): jax.lax.all_to_all(far_arr, axis_name=comm_axis, split_axis=0, concat_axi...]
    another operation x0 -> x3, local copies, waits for them, and re-layouts: none -> 23.2 us  [the longest x2 21.3 us: blocks(): return piece.reshape(-1, CLUSTER_MOMENTUM, extent)]
    reshape x3 -> x1, local copies, waits for them, and re-layouts: 37.5 us -> 15.4 us  [blocks(): return piece.reshape(-1, CLUSTER_MOMENTUM, extent)]
    all_to_all x0 -> x1, starting transfers between devices: none -> 13.5 us  [resolve_record_by_axis(): jax.lax.all_to_all(far_arr, axis_name=comm_axis, split_axis=0, concat_axi...]
    unnamed x6 -> x5, waiting for transfers between devices: 727 us -> 727 us
  transfers between devices with their start and end apart: 4 -> 4, of which waited for: 4 -> 4; matrix products, arithmetic and copies ran while one was open for 2% -> 3% of each run, Pallas kernels for 0% -> 0%
where the time goes in v1:
time: 923 us
  waiting for transfers between devices  818 us (89%)
  local copies, waits for them, and re-layouts  47.1 us (5%)
  between operations  15.3 us (2%)
  starting transfers between devices  14 us (2%)
  blocking collectives  13.4 us (1%)
  matrix products  10.3 us (1%)
    unnamed x5, waiting for transfers between devices  727 us
    all_to_all x1, waiting for transfers between devices, resolve_record_by_axis(): jax.lax.all_to_all(far_arr, axis_name=comm_axis, split_axis=0, concat_axi...  46 us
    all_gather x1, waiting for transfers between devices, shards(): lax.all_gather(up_all, 'walker', axis=0, tiled=True)  44.5 us
    another operation x2, local copies, waits for them, and re-layouts, blocks(): return piece.reshape(-1, CLUSTER_MOMENTUM, extent)  21.3 us
  transfers between devices with their start and end apart: 4, of which 4 were waited for; matrix products, arithmetic and copies ran while one was open for 3% of the time, Pallas kernels for 0%

profile of v1, /device:TPU:2, one launch (start us, length us, event | category | flops | bytes accessed | tf_op | source)
XLA Modules:
  0.0 922.6 jit_solution(3342087112266298839)
XLA Ops:
  7.2 5.7 all_gather.13
  12.9 2.0 stack.2
  14.9 0.0 copy-start.1
  14.9 13.5 %all-to-all-start = ((bf16[64,1,1,4,4288]{4,3,2,1,0:T(4,128)(2,1)}), bf16[64,1,1,4,4288]{4,3,2,1,0:T(4,128)(2,1)S(1)}, u32[]{:S(2)}, u32[]{:S(2)}) async-start(bf16[64,1,1,4,4288]{4,3,2,1,0:T(4,128)(2,1)} %stack.2), calls=%async_computation | async-start | bytes 4456448 | tf_op jit(solution)/shard_map/all_to_all | solution.py:56
  28.4 0.0 all-gather.2.cloned.1.call-start
  28.5 0.0 copy-done.1
  28.5 7.7 all_gather.11
  36.2 0.6 copy.23
  36.8 0.0 all-gather.2.cloned.1.call-update
  36.8 0.2 reduce-scatter.7.cloned.1.call-start
  38.5 46.0 %all-to-all-done = bf16[64,1,1,4,4288]{4,3,2,1,0:T(4,128)(2,1)S(1)} async-done(((bf16[64,1,1,4,4288]{4,3,2,1,0:T(4,128)(2,1)}), bf16[64,1,1,4,4288]{4,3,2,1,0:T(4,128)(2,1)S(1)}, u32[]{:S(2)}, u32[]{:S(2)}) %all-to-all-start) | async-done | bytes 2195488 | tf_op jit(solution)/shard_map/all_to_all | solution.py:56
  84.6 14.8 %reshape_reshape.3 = bf16[256,64,67]{2,1,0:T(8,128)(2,1)} reshape(bf16[64,1,1,4,4288]{4,3,2,1,0:T(4,128)(2,1)S(1)} %all-to-all-done) | data formatting | bytes 4390912 | tf_op jit(solution)/shard_map/reshape;reshape | solution.py:48
  99.3 6.5 copy.27
  105.9 2.1 gather_fusion.1
  108.0 2.1 gather_fusion
  110.1 2.9 select_bitcast_fusion
  113.0 1.3 multiply_convert_fusion
  114.2 44.5 %all-gather.2.cloned.1.call-done = bf16[64,1,4,4288]{3,2,1,0:T(4,128)(2,1)} async-done(((bf16[1,1,4,4288]{3,2,1,0:T(4,128)(2,1)}), bf16[64,1,4,4288]{3,2,1,0:T(4,128)(2,1)}) %all-gather.2.cloned.1.call-update) | async-done | bytes 2195472 | tf_op jit(solution)/shard_map/all_gather | solution.py:51
  158.8 15.4 %reshape.59 = bf16[256,64,67]{2,1,0:T(8,128)(2,1)} reshape(bf16[64,1,4,4288]{3,2,1,0:T(4,128)(2,1)} %all-gather.2.cloned.1.call-done) | data formatting | bytes 4390912 | tf_op jit(solution)/shard_map/reshape | solution.py:48
  174.2 0.0 copy-start.2
  174.2 1.5 constant_dynamic-slice_fusion.1
  175.7 0.2 constant_dynamic-slice_fusion.2
  175.9 0.1 copy.37
  176.0 0.1 copy.36
  176.1 0.8 convolution_multiply_fusion
  176.9 0.0 copy-done.2
  176.9 0.0 copy-start
  176.9 4.8 convolution_bitcast_fusion.1
  181.7 0.0 reduce-scatter.7.cloned.1.call-update
  181.7 0.3 reduce-scatter.9.cloned.1.call-start
  182.0 365.7 %reduce-scatter.7.cloned.1.call-done = f32[64,1]{1,0:T(8,128)} async-done(((f32[4096,1]{1,0:T(8,128)}), f32[64,1]{1,0:T(8,128)}) %reduce-scatter.7.cloned.1.call-update) | async-done | bytes 272
  547.7 0.8 copy.30
  548.5 0.0 copy-done
  548.5 4.8 convolution_bitcast_fusion
  553.3 0.0 reduce-scatter.9.cloned.1.call-update
  553.3 361.5 %reduce-scatter.9.cloned.1.call-done = f32[64,1]{1,0:T(8,128)} async-done(((f32[4096,1]{1,0:T(8,128)}), f32[64,1]{1,0:T(8,128)}) %reduce-scatter.9.cloned.1.call-update) | async-done | bytes 272
  914.8 0.8 copy.32
  915.6 0.5 fusion.14
  (6 shorter events, 0.1 us)
Async XLA Ops:
  14.9 13.6 %copy-start.1 = (bf16[1,1,1,4288]{3,2,1,0:T(2,128)(2,1)S(1)}, bf16[1,1,1,4288]{3,2,1,0:T(2,128)(2,1)}, u32[]{:S(2)}) copy-start(bf16[1,1,1,4288]{3,2,1,0:T(2,128)(2,1)} %param.9) | copy-start | bytes 25732
  14.9 69.7 %all-to-all-start = ((bf16[64,1,1,4,4288]{4,3,2,1,0:T(4,128)(2,1)}), bf16[64,1,1,4,4288]{4,3,2,1,0:T(4,128)(2,1)S(1)}, u32[]{:S(2)}, u32[]{:S(2)}) async-start(bf16[64,1,1,4,4288]{4,3,2,1,0:T(4,128)(2,1)} %stack.2), calls=%async_computation | async-start | bytes 4456448 | tf_op jit(solution)/shard_map/all_to_all | solution.py:56
  28.4 130.4 %all-gather.2.cloned.1.call-start = ((), (), s32[]{:S(2)}) async-start(), calls=%async_computation.3 | async-start | bytes 2263040 | tf_op jit(solution)/shard_map/all_gather | solution.py:51
  36.8 510.8 %reduce-scatter.7.cloned.1.call-start = ((), (), s32[]{:S(2)}) async-start(), calls=%async_computation.4 | async-start | bytes 2129920
  174.2 2.7 copy-start.2
  176.9 371.6 %copy-start = (f32[64,4096]{1,0:T(8,128)}, f32[64,4096]{1,0:T(8,128)S(1)}, u32[]{:S(2)}) copy-start(f32[64,4096]{1,0:T(8,128)S(1)} %convolution_multiply_fusion) | copy-start | bytes 3145732
  181.7 733.1 %reduce-scatter.9.cloned.1.call-start = ((), (), s32[]{:S(2)}) async-start(), calls=%async_computation.5 | async-start | bytes 2129920
Sparse Core Ops, SparseCore 0:
  37.0 121.7 all-gather.1
  181.8 365.8 reduce-scatter.6
  553.4 361.2 reduce-scatter.8
